TPU v7x, 256 devices: a whole 4x4x8 slice. The times are simulated.
256 devices in a mesh: prow: 16 (over x, y), pcol: 16 (over z, core).
Axes of the slice: x: 4, y: 4, z: 8, core: 2. Of those that a mesh axis runs over, the one named last changes fastest.
Arguments:
- ainv: float32 [16384, 16384], P('prow', 'pcol'), as said below
- panels: float32 [3, 16384, 512], P(None, 'prow', 'pcol'), may hold values from -0.53 to 0.53
- pattern: int32 [3, 128], replicated, may hold values 0 or 1
- coupling: float32 [3, 512, 512], replicated, may hold values from -0.25 to 0.25
- dinv: float32 [3, 512, 512], replicated, as said below
Outputs:
- xpanel: float32 [3, 16384, 512], P(None, 'prow', 'pcol')
- xcross: float32 [3, 512, 512], P(None, 'pcol')
- ydiag: float32 [3, 512, 512], P(None, 'pcol')
Inputs may be any that keep to these rules, and one draw needn't show every extreme that they name: ainv is symmetric: ainv equals its transpose up to rounding. Each dinv[k] is symmetric: it equals its transpose exactly.
All inputs are finite; a program needn't handle non-finite values.
Results may differ from a plain program's by a relative error of at most 0.000092.
Values sent between devices are 32-bit elements; how exact they have to be, the bound alone decides.
A program may use at most 128 MiB of HBM per device.

v0:
```python
import jax
import jax.numpy as jnp
from jax import lax
from jax.sharding import PartitionSpec as P

NB = 128
high = lax.Precision.HIGH
highest = lax.Precision.HIGHEST


def mm(left, right, precision=high):
    return jnp.dot(left, right, precision=precision, preferred_element_type=jnp.float32)


def tmm(left, right, precision=high):
    return lax.dot_general(
        left,
        right,
        (((0,), (0,)), ((), ())),
        precision=precision,
        preferred_element_type=jnp.float32,
    )


def mmt(left, right, precision=high):
    return lax.dot_general(
        left,
        right,
        (((1,), (1,)), ((), ())),
        precision=precision,
        preferred_element_type=jnp.float32,
    )


def shards(ainv, panels, pattern, coupling, dinv):
    rows = lax.axis_size("prow")
    cols = lax.axis_size("pcol")
    row_index = lax.axis_index("prow")
    col_index = lax.axis_index("pcol")
    count, depth, width = panels.shape
    blocks_here = depth // NB
    flags = lax.dynamic_slice_in_dim(pattern, row_index * blocks_here, blocks_here, 1)
    row_mask = jnp.repeat(flags.astype(jnp.float32), NB, axis=1)
    factors = jnp.swapaxes(panels, 1, 2) * row_mask[:, None, :]
    f0, f1, f2 = lax.all_gather(factors, "pcol", axis=1, tiled=True)
    c0, c1, c2 = (coupling[0], coupling[1], coupling[2])
    u01 = -c0
    u12 = -c2
    u02 = mm(c0, c2, highest) - c1
    h0 = f0
    h1 = f1 + tmm(u01, f0)
    h2 = f2 + tmm(u02, f0) + tmm(u12, f1)
    ht = jnp.concatenate([h0, h1, h2], 0)
    partial = mm(ht, ainv).reshape(count, rows, width, depth)
    mine = lax.psum_scatter(partial, "prow", scatter_dimension=1, tiled=False)
    perm = [(r * cols + c, c * cols + r) for r in range(rows) for c in range(cols)]
    xt = -lax.ppermute(mine, ("prow", "pcol"), perm)
    inner0 = mmt(xt[0], ht)
    inner1 = mmt(xt[1], ht[512:])
    inner2 = mmt(xt[2], ht[1024:])
    summed = lax.psum(jnp.concatenate([inner0, inner1, inner2], 1), "prow")
    start = col_index * width

    def own(matrix, axis):
        return lax.dynamic_slice_in_dim(matrix, start, width, axis)

    d0 = own(dinv[0], 0)
    a01 = tmm(own(u01, 1), dinv[0], highest)
    a02 = tmm(own(u02, 1), dinv[0], highest)
    b1 = own(dinv[1], 0)
    b12 = tmm(own(u12, 1), dinv[1], highest)
    y0 = d0 - summed[:, 0:512]
    e01 = mm(d0, u01, highest) - summed[:, 512:1024]
    e02 = mm(d0, u02, highest) - summed[:, 1024:1536]
    y1 = b1 + mm(a01, u01, highest) - summed[:, 1536:2048]
    e12 = mm(a01, u02, highest) + mm(b1, u12, highest) - summed[:, 2048:2560]
    y2 = own(dinv[2], 0) + mm(a02, u02, highest) + mm(b12, u12, highest) - summed[:, 2560:3072]
    return (jnp.swapaxes(xt, 1, 2), jnp.stack([e01, e02, e12], 0), jnp.stack([y0, y1, y2], 0))


def solution(mesh):
    placed = (P("prow", "pcol"), P(None, "prow", "pcol"), P(), P(), P())
    return jax.shard_map(
        shards,
        mesh=mesh,
        in_specs=placed,
        out_specs=(P(None, "prow", "pcol"), P(None, "pcol", None), P(None, "pcol", None)),
        check_vma=False,
    )
```

profile of v0, /device:TPU:2, one launch (start us, length us, event | category | flops | bytes accessed | tf_op | source)
XLA Modules:
  0.0 337.9 jit_solution(12168469248919959419)
XLA Ops:
  8.1 1.8 multiply_bitcast_fusion
  11.3 4.8 %convolution_subtract_fusion = f32[512,512]{0,1:T(8,128)} fusion(f32[1,512,512]{1,2,0:T(8,128)} %copy.12, f32[3,512,512]{2,1,0:T(8,128)} %param.8), kind=kOutput, calls=%fused_computation.14 | convolution fusion | flops 1610874880 | bytes 4194304 | tf_op jit(solution)/shard_map/dot_general | solution.py:12
  16.1 43.3 %all-gather.2.cloned.1.call-done = f32[3,512,1024]{2,1,0:T(8,128)} async-done(((f32[3,32,1024]{2,1,0:T(8,128)}), f32[3,512,1024]{2,1,0:T(8,128)}) %all-gather.2.cloned.1.call-update) | async-done | bytes 6291472 | tf_op jit(solution)/shard_map/all_gather | solution.py:45
  59.4 4.3 %bitcast_add_fusion = f32[512,1024]{1,0:T(8,128)S(1)} fusion(f32[3,512,1024]{2,1,0:T(8,128)} %all-gather.2.cloned.1.call-done, f32[3,512,512]{2,1,0:T(8,128)S(1)} %copy-done), kind=kOutput, calls=%fused_computation.12 | convolution fusion | flops 1611399168 | bytes 7340032 | tf_op jit(solution)/shard_map/dot_general | solution.py:16
  63.7 4.0 %slice_bitcast_fusion.2 = f32[512,1024]{1,0:T(8,128)} fusion(f32[3,512,1024]{2,1,0:T(8,128)} %all-gather.2.cloned.1.call-done), kind=kLoop, calls=%fused_computation.11 | loop fusion | bytes 4194304 | tf_op jit(solution)/shard_map/unstack | solution.py:45
  67.7 1.9 fusion.62
  69.7 2.0 fusion.7
  71.8 16.0 %fusion.1 = f32[1536,1024]{1,0:T(8,128)S(1)} fusion(f32[1024,1024]{1,0:T(8,128)} %param.5, f32[512,1024]{1,0:T(8,128)S(1)} %fusion.7, f32[512,1024]{1,0:T(8,128)S(1)} %bitcast_add_fusion, f32[512,1024]{1,0:T(8,128)} %slice_bitcast_fusion.2), kind=kOutput, calls=%fused_computation.2 | convolution fusion | flops 9666822144 | bytes 16777216 | tf_op jit(solution)/shard_map/dot_general | solution.py:12
  87.8 3.2 copy.11
  92.4 2.0 fusion.21
  95.4 81.0 %reduce-scatter.4.cloned.1.call-done = f32[3,1,32,1024]{3,2,0,1:T(8,128)} async-done(((f32[3,16,32,1024]{3,2,0,1:T(8,128)}), f32[3,1,32,1024]{3,2,0,1:T(8,128)}) %reduce-scatter.4.cloned.1.call-update) | async-done | bytes 393232
  176.5 5.0 %collective-permute-start = (f32[3,32,1024]{2,1,0:T(8,128)}, f32[3,32,1024]{2,1,0:T(8,128)S(1)}, u32[]{:S(2)}, u32[]{:S(2)}) collective-permute-start(f32[3,32,1024]{2,1,0:T(8,128)} %bitcast.108), channel_id=1, source_target_pairs={{0,0},{1,16},{2,32},{3,48},{4,64},{5,80},{6,96},{7,112},{8,128},{9... | collective-permute-start | bytes 1179656 | tf_op jit(solution)/shard_map/ppermute | solution.py:57
  181.4 2.0 fusion.19
  183.4 3.7 %fusion.63 = (f32[1,512,512]{2,1,0:T(8,128)}, f32[1,512,512]{2,1,0:T(8,128)}, f32[1,512,512]{2,1,0:T(8,128)}) fusion(f32[3,512,512]{2,1,0:T(8,128)} %param.9), kind=kLoop, calls=%fused_computation.89 | loop fusion | bytes 6291456 | tf_op jit(solution)/shard_map/slice | solution.py:77
  187.2 29.7 %collective-permute-done = f32[3,32,1024]{2,1,0:T(8,128)S(1)} collective-permute-done((f32[3,32,1024]{2,1,0:T(8,128)}, f32[3,32,1024]{2,1,0:T(8,128)S(1)}, u32[]{:S(2)}, u32[]{:S(2)}) %collective-permute-start) | collective-permute-done | bytes 393248 | tf_op jit(solution)/shard_map/ppermute | solution.py:57
  217.6 3.0 fusion
  220.6 2.0 fusion.2
  224.5 2.1 fusion.17
  226.6 2.3 convolution_add_fusion.1
  228.8 92.2 %all-reduce.3.cloned.1.call-done = f32[32,3072]{1,0:T(8,128)} async-done(((f32[32,3072]{1,0:T(8,128)}), f32[32,3072]{1,0:T(8,128)}) %all-reduce.3.cloned.1.call-update) | async-done | bytes 393232 | tf_op jit(solution)/shard_map/psum | solution.py:61
  321.0 2.3 fusion.15
  323.3 1.6 fusion.16
  325.8 1.6 fusion.12
  327.4 1.6 fusion.14
  (38 shorter events, 10.6 us)
Async XLA Ops:
  7.2 2.8 slice-start
  7.2 52.3 %all-gather.2.cloned.1.call-start = ((), (), s32[]{:S(2)}) async-start(), calls=%async_computation.1 | async-start | bytes 6684672 | tf_op jit(solution)/shard_map/all_gather | solution.py:45
  10.0 166.5 %reduce-scatter.4.cloned.1.call-start = ((), (), s32[]{:S(2)}) async-start(), calls=%async_computation.3 | async-start | bytes 6684672
  11.3 48.1 %copy-start = (f32[3,512,512]{2,1,0:T(8,128)S(1)}, f32[3,512,512]{2,1,0:T(8,128)}, u32[]{:S(2)}) copy-start(f32[3,512,512]{2,1,0:T(8,128)} %param.8) | copy-start | bytes 9437188
  59.4 8.3 %copy-start.5 = (f32[3,512,1024]{2,1,0:T(8,128)S(1)}, f32[3,512,1024]{2,1,0:T(8,128)}, u32[]{:S(2)}) copy-start(f32[3,512,1024]{2,1,0:T(8,128)} %all-gather.2.cloned.1.call-done) | copy-start | bytes 18874372
  63.7 8.0 %copy-start.6 = (f32[512,1024]{1,0:T(8,128)}, f32[512,1024]{1,0:T(8,128)S(1)}, u32[]{:S(2)}) copy-start(f32[512,1024]{1,0:T(8,128)S(1)} %bitcast_add_fusion) | copy-start | bytes 6291460
  63.7 4.0 %copy-start.1 = (f32[512,512]{0,1:T(8,128)S(1)}, f32[512,512]{0,1:T(8,128)}, u32[]{:S(2)}) copy-start(f32[512,512]{0,1:T(8,128)} %convolution_subtract_fusion) | copy-start | bytes 3145732
  71.7 16.0 %copy-start.3 = (f32[512,1024]{1,0:T(8,128)}, f32[512,1024]{1,0:T(8,128)S(1)}, u32[]{:S(2)}) copy-start(f32[512,1024]{1,0:T(8,128)S(1)} %fusion.7) | copy-start | bytes 6291460
  91.1 229.9 %all-reduce.3.cloned.1.call-start = ((), (), s32[]{:S(2)}) async-start(), calls=%async_computation.2 | async-start | bytes 786432 | tf_op jit(solution)/shard_map/psum | solution.py:61
  91.1 3.2 copy-start.2
  176.5 40.4 %collective-permute-start = (f32[3,32,1024]{2,1,0:T(8,128)}, f32[3,32,1024]{2,1,0:T(8,128)S(1)}, u32[]{:S(2)}, u32[]{:S(2)}) collective-permute-start(f32[3,32,1024]{2,1,0:T(8,128)} %bitcast.108), channel_id=1, source_target_pairs={{0,0},{1,16},{2,32},{3,48},{4,64},{5,80},{6,96},{7,112},{8,128},{9... | collective-permute-start | bytes 1179656 | tf_op jit(solution)/shard_map/ppermute | solution.py:57
  183.4 34.2 %copy-start.4 = (f32[512,1024]{1,0:T(8,128)S(1)}, f32[512,1024]{1,0:T(8,128)}, u32[]{:S(2)}) copy-start(f32[512,1024]{1,0:T(8,128)} %copy-done.3) | copy-start | bytes 6291460
  183.4 34.2 %copy-start.7 = (f32[512,1024]{1,0:T(8,128)S(1)}, f32[512,1024]{1,0:T(8,128)}, u32[]{:S(2)}) copy-start(f32[512,1024]{1,0:T(8,128)} %copy-done.6) | copy-start | bytes 6291460
  183.4 34.2 %copy-start.8 = (f32[512,1024]{1,0:T(8,128)S(1)}, f32[512,1024]{1,0:T(8,128)}, u32[]{:S(2)}) copy-start(f32[512,1024]{1,0:T(8,128)} %slice_bitcast_fusion.2) | copy-start | bytes 6291460
Sparse Core Ops, SparseCore 0:
  10.4 48.9 all-gather.1
  91.2 85.2 reduce-scatter.3
  224.6 96.3 all-reduce.2
where the time goes:
time: 338 us
  waiting for transfers between devices  246 us (73%)
  matrix products  53.1 us (16%)
  between operations  14 us (4%)
  local copies, waits for them, and re-layouts  12.4 us (4%)
  other arithmetic  7.1 us (2%)
  starting transfers between devices  5.08 us (2%)
    psum x1, waiting for transfers between devices, shards(): summed = lax.psum(jnp.concatenate([inner0, inner1, inner2], 1), 'prow')  92.2 us
    unnamed x4, waiting for transfers between devices  81.1 us
    all_gather x1, waiting for transfers between devices, shards(): f0, f1, f2 = lax.all_gather(factors, 'pcol', axis=1, tiled=True)  43.3 us
    dot_general x9, matrix products, mm(): jnp.dot(left, right, precision=precision, preferred_element_type=jnp.floa...  32.8 us
    ppermute x1, waiting for transfers between devices, shards(): xt = -lax.ppermute(mine, ('prow', 'pcol'), perm)  29.7 us
    dot_general x6, matrix products, tmm(): lax.dot_general(left, right, (((0,), (0,)), ((), ())), precision=precisio...  14.2 us
  transfers between devices with their start and end apart: 4, of which 4 were waited for; matrix products, arithmetic and copies ran while one was open for 6% of the time, Pallas kernels for 0%

commit v1 on v0

--- a/solution.py
+++ b/solution.py
@@ -58,7 +58,7 @@
     inner0 = mmt(xt[0], ht)
     inner1 = mmt(xt[1], ht[512:])
     inner2 = mmt(xt[2], ht[1024:])
-    summed = lax.psum(jnp.concatenate([inner0, inner1, inner2], 1), "prow")
+    summed = jnp.sum(lax.all_gather(jnp.concatenate([inner0, inner1, inner2], 1), "prow"), axis=0)
     start = col_index * width
 
     def own(matrix, axis):

time: 338 us -> 316 us (0.935)
  waiting for transfers between devices: 246 us -> 223 us
    psum x1 -> x0, waiting for transfers between devices: 92.2 us -> none  [shards(): summed = lax.psum(jnp.concatenate([inner0, inner1, inner2], 1), 'prow')]
    all_gather x0 -> x1, waiting for transfers between devices: none -> 58.7 us  [shards(): lax.all_gather(jnp.concatenate([inner0, inner1, inner2], 1), 'prow')]
    ppermute x1, waiting for transfers between devices: 29.7 us -> 35.4 us  [shards(): xt = -lax.ppermute(mine, ('prow', 'pcol'), perm)]
    unnamed x4, waiting for transfers between devices: 81.1 us -> 85.4 us
  transfers between devices with their start and end apart: 4 -> 4, of which waited for: 4 -> 4; matrix products, arithmetic and copies ran while one was open for 6% -> 5% of each run, Pallas kernels for 0% -> 0%
where the time goes in v1:
time: 316 us; the launch traced here: 315 us
  waiting for transfers between devices  223 us (71%)
  matrix products  53.5 us (17%)
  between operations  14 us (4%)
  local copies, waits for them, and re-layouts  10.4 us (3%)
  other arithmetic  9.2 us (3%)
  starting transfers between devices  5.09 us (2%)
    unnamed x4, waiting for transfers between devices  85.4 us
    all_gather x1, waiting for transfers between devices, shards(): lax.all_gather(jnp.concatenate([inner0, inner1, inner2], 1), 'prow')  58.7 us
    all_gather x1, waiting for transfers between devices, shards(): f0, f1, f2 = lax.all_gather(factors, 'pcol', axis=1, tiled=True)  43.1 us
    ppermute x1, waiting for transfers between devices, shards(): xt = -lax.ppermute(mine, ('prow', 'pcol'), perm)  35.4 us
    dot_general x9, matrix products, mm(): jnp.dot(left, right, precision=precision, preferred_element_type=jnp.floa...  32.1 us
    dot_general x6, matrix products, tmm(): lax.dot_general(left, right, (((0,), (0,)), ((), ())), precision=precisio...  12.5 us
    dot_general x3, matrix products, mmt(): lax.dot_general(left, right, (((1,), (1,)), ((), ())), precision=precisio...  8.89 us
  transfers between devices with their start and end apart: 4, of which 4 were waited for; matrix products, arithmetic and copies ran while one was open for 5% of the time, Pallas kernels for 0%

profile of v1, /device:TPU:2, one launch (start us, length us, event | category | flops | bytes accessed | tf_op | source)
XLA Modules:
  0.0 314.9 jit_solution(870340734652080694)
XLA Ops:
  8.1 1.8 multiply_bitcast_fusion
  11.4 4.9 %convolution_subtract_fusion = f32[512,512]{0,1:T(8,128)} fusion(f32[1,512,512]{1,2,0:T(8,128)} %copy.12, f32[3,512,512]{2,1,0:T(8,128)} %param.8), kind=kOutput, calls=%fused_computation.14 | convolution fusion | flops 1610874880 | bytes 4194304 | tf_op jit(solution)/shard_map/dot_general | solution.py:12
  16.3 43.1 %all-gather.4.cloned.1.call-done = f32[3,512,1024]{2,1,0:T(8,128)} async-done(((f32[3,32,1024]{2,1,0:T(8,128)}), f32[3,512,1024]{2,1,0:T(8,128)}) %all-gather.4.cloned.1.call-update) | async-done | bytes 6291472 | tf_op jit(solution)/shard_map/all_gather | solution.py:45
  59.4 4.3 %bitcast_add_fusion = f32[512,1024]{1,0:T(8,128)S(1)} fusion(f32[3,512,1024]{2,1,0:T(8,128)} %all-gather.4.cloned.1.call-done, f32[3,512,512]{2,1,0:T(8,128)S(1)} %copy-done), kind=kOutput, calls=%fused_computation.12 | convolution fusion | flops 1611399168 | bytes 7340032 | tf_op jit(solution)/shard_map/dot_general | solution.py:16
  63.7 4.0 %slice_bitcast_fusion.2 = f32[512,1024]{1,0:T(8,128)} fusion(f32[3,512,1024]{2,1,0:T(8,128)} %all-gather.4.cloned.1.call-done), kind=kLoop, calls=%fused_computation.11 | loop fusion | bytes 4194304 | tf_op jit(solution)/shard_map/unstack | solution.py:45
  67.8 1.9 fusion.62
  69.7 2.0 fusion.7
  71.8 16.0 %fusion.1 = f32[1536,1024]{1,0:T(8,128)S(1)} fusion(f32[1024,1024]{1,0:T(8,128)} %param.5, f32[512,1024]{1,0:T(8,128)S(1)} %fusion.7, f32[512,1024]{1,0:T(8,128)S(1)} %bitcast_add_fusion, f32[512,1024]{1,0:T(8,128)} %slice_bitcast_fusion.2), kind=kOutput, calls=%fused_computation.2 | convolution fusion | flops 9666822144 | bytes 16777216 | tf_op jit(solution)/shard_map/dot_general | solution.py:12
  87.8 3.2 %copy.11 = f32[3,16,32,1024]{3,2,0,1:T(8,128)} copy(f32[3,16,32,1024]{3,2,1,0:T(8,128)S(1)} %bitcast.107) | data formatting | bytes 12582912 | tf_op jit(solution)/shard_map/reshape | solution.py:54
  91.1 85.3 %reduce-scatter.4.cloned.1.call-done = f32[3,1,32,1024]{3,2,0,1:T(8,128)} async-done(((f32[3,16,32,1024]{3,2,0,1:T(8,128)}), f32[3,1,32,1024]{3,2,0,1:T(8,128)}) %reduce-scatter.4.cloned.1.call-update) | async-done | bytes 393232
  176.4 5.0 %collective-permute-start = (f32[3,32,1024]{2,1,0:T(8,128)}, f32[3,32,1024]{2,1,0:T(8,128)S(1)}, u32[]{:S(2)}, u32[]{:S(2)}) collective-permute-start(f32[3,32,1024]{2,1,0:T(8,128)} %bitcast.110), channel_id=1, source_target_pairs={{0,0},{1,16},{2,32},{3,48},{4,64},{5,80},{6,96},{7,112},{8,128},{9... | collective-permute-start | bytes 1179656 | tf_op jit(solution)/shard_map/ppermute | solution.py:57
  181.4 35.4 %collective-permute-done = f32[3,32,1024]{2,1,0:T(8,128)S(1)} collective-permute-done((f32[3,32,1024]{2,1,0:T(8,128)}, f32[3,32,1024]{2,1,0:T(8,128)S(1)}, u32[]{:S(2)}, u32[]{:S(2)}) %collective-permute-start) | collective-permute-done | bytes 393248 | tf_op jit(solution)/shard_map/ppermute | solution.py:57
  217.6 5.8 %fusion = f32[32,1536]{1,0:T(8,128)S(1)} fusion(f32[512,1024]{1,0:T(8,128)} %copy-done.3, f32[512,1024]{1,0:T(8,128)} %copy-done.7, f32[512,1024]{1,0:T(8,128)} %slice_bitcast_fusion.2, f32[3,32,1024]{2,1,0:T(8,128)S(1)} %get-tuple-element.8), kind=kOutput, calls=%fused_computation.1 | convolution fusion | flops 305135616 | bytes 6619136 | tf_op jit(solution)/shard_map/dot_general | solution.py:26
  223.5 2.0 fusion.2
  227.4 2.1 fusion.19
  231.9 1.7 fusion.65
  233.6 1.6 fusion.63
  235.3 1.7 convolution_add_fusion.1
  236.9 58.7 %all-gather.6.cloned.1.call-done = f32[512,3072]{1,0:T(8,128)} async-done(((f32[32,3072]{1,0:T(8,128)}), f32[512,3072]{1,0:T(8,128)}) %all-gather.6.cloned.1.call-update) | async-done | bytes 6291472 | tf_op jit(solution)/shard_map/all_gather | solution.py:61
  295.7 3.1 reduce_sum.9
  298.8 2.4 fusion.15
  301.2 1.6 fusion.16
  303.6 1.6 fusion.12
  305.3 1.6 fusion.14
  (47 shorter events, 9.9 us)
Async XLA Ops:
  7.2 2.8 slice-start
  7.2 52.3 %all-gather.4.cloned.1.call-start = ((), (), s32[]{:S(2)}) async-start(), calls=%async_computation.1 | async-start | bytes 6684672 | tf_op jit(solution)/shard_map/all_gather | solution.py:45
  10.0 166.5 %reduce-scatter.4.cloned.1.call-start = ((), (), s32[]{:S(2)}) async-start(), calls=%async_computation.3 | async-start | bytes 6684672
  11.4 48.1 %copy-start = (f32[3,512,512]{2,1,0:T(8,128)S(1)}, f32[3,512,512]{2,1,0:T(8,128)}, u32[]{:S(2)}) copy-start(f32[3,512,512]{2,1,0:T(8,128)} %param.8) | copy-start | bytes 9437188
  59.4 8.3 %copy-start.6 = (f32[3,512,1024]{2,1,0:T(8,128)S(1)}, f32[3,512,1024]{2,1,0:T(8,128)}, u32[]{:S(2)}) copy-start(f32[3,512,1024]{2,1,0:T(8,128)} %all-gather.4.cloned.1.call-done) | copy-start | bytes 18874372
  63.7 8.0 %copy-start.7 = (f32[512,1024]{1,0:T(8,128)}, f32[512,1024]{1,0:T(8,128)S(1)}, u32[]{:S(2)}) copy-start(f32[512,1024]{1,0:T(8,128)S(1)} %bitcast_add_fusion) | copy-start | bytes 6291460
  63.7 4.0 %copy-start.1 = (f32[512,512]{0,1:T(8,128)S(1)}, f32[512,512]{0,1:T(8,128)}, u32[]{:S(2)}) copy-start(f32[512,512]{0,1:T(8,128)} %convolution_subtract_fusion) | copy-start | bytes 3145732
  71.8 16.0 %copy-start.3 = (f32[512,1024]{1,0:T(8,128)}, f32[512,1024]{1,0:T(8,128)S(1)}, u32[]{:S(2)}) copy-start(f32[512,1024]{1,0:T(8,128)S(1)} %fusion.7) | copy-start | bytes 6291460
  91.1 204.6 %all-gather.6.cloned.1.call-start = ((), (), s32[]{:S(2)}) async-start(), calls=%async_computation.2 | async-start | bytes 6684672 | tf_op jit(solution)/shard_map/all_gather | solution.py:61
  176.4 40.4 %collective-permute-start = (f32[3,32,1024]{2,1,0:T(8,128)}, f32[3,32,1024]{2,1,0:T(8,128)S(1)}, u32[]{:S(2)}, u32[]{:S(2)}) collective-permute-start(f32[3,32,1024]{2,1,0:T(8,128)} %bitcast.110), channel_id=1, source_target_pairs={{0,0},{1,16},{2,32},{3,48},{4,64},{5,80},{6,96},{7,112},{8,128},{9... | collective-permute-start | bytes 1179656 | tf_op jit(solution)/shard_map/ppermute | solution.py:57
  217.6 5.8 %copy-start.4 = (f32[512,1024]{1,0:T(8,128)S(1)}, f32[512,1024]{1,0:T(8,128)}, u32[]{:S(2)}) copy-start(f32[512,1024]{1,0:T(8,128)} %copy-done.3) | copy-start | bytes 6291460
  217.6 5.8 %copy-start.8 = (f32[512,1024]{1,0:T(8,128)S(1)}, f32[512,1024]{1,0:T(8,128)}, u32[]{:S(2)}) copy-start(f32[512,1024]{1,0:T(8,128)} %copy-done.7) | copy-start | bytes 6291460
  227.4 2.4 copy-start.5
  229.6 2.4 copy-start.2
  230.6 1.4 copy-start.9
  298.8 6.4 %copy-start.11 = (f32[32,512]{1,0:T(8,128)S(1)}, f32[32,512]{1,0:T(8,128)}, u32[]{:S(2)}) copy-start(f32[32,512]{1,0:T(8,128)} %fusion.65) | copy-start | bytes 196612
  298.8 8.0 %copy-start.10 = (f32[32,512]{1,0:T(8,128)S(1)}, f32[32,512]{1,0:T(8,128)}, u32[]{:S(2)}) copy-start(f32[32,512]{1,0:T(8,128)} %fusion.17) | copy-start | bytes 196612
  298.8 8.0 %copy-start.12 = (f32[32,512]{1,0:T(8,128)S(1)}, f32[32,512]{1,0:T(8,128)}, u32[]{:S(2)}) copy-start(f32[32,512]{1,0:T(8,128)} %convolution_add_fusion.1) | copy-start | bytes 196612
Sparse Core Ops, SparseCore 0:
  10.4 48.9 all-gather.3
  91.2 85.1 reduce-scatter.3
  227.5 68.1 all-gather.5
